TPU v7x, 256 devices: a whole 4x4x8 slice. The times are simulated.
256 devices in a mesh: member: 4 (over x), vol: 64 (over z, y, core).
Axes of the slice: x: 4, y: 4, z: 8, core: 2. Of those that a mesh axis runs over, the one named last changes fastest.
Arguments:
- features: bfloat16 [32, 1024, 32, 128], P(None, 'vol'), may hold values from -6 to 6
- corner_z: int32 [64, 4], P('vol'), may hold values from 0 to 15, as said below
- corner_y: int32 [64, 4], P('vol'), may hold values from 0 to 24
- counts: int32 [64], P('vol'), may hold values from 0 to 4, as said below
- conv_w: bfloat16 [4, 32, 32, 3, 3, 3], P('member'), may hold values from -0.21875 to 0.21875
- norm_gain: float32 [4, 32], P('member'), may hold values from 0.1 to 1.9
- norm_shift: float32 [4, 32], P('member'), may hold values from -3 to 3
- seg_w: bfloat16 [4, 3, 32], P('member'), may hold values from -1 to 1
- seg_b: float32 [4, 3], P('member'), may hold values from -4 to 4
Outputs:
- probabilities: float32 [3, 1024, 32, 128], P(None, 'vol', 'member')
Inputs may be any that keep to these rules, and one draw needn't show every extreme that they name: counts of slab s and slab s + 32 sum to exactly 4; slab 1 holds 4. `corner_z`: slot 0 of every slab has its corner at plane 16 - 1.
All inputs are finite; a program needn't handle non-finite values.
Results may differ from a plain program's by a relative error of at most 0.00059.
Values may be sent and summed in bfloat16 or wider, within the bound.
A program may use at most 128 MiB of HBM per device.

v0:
```python
import functools

import jax
import jax.numpy as jnp
import numpy as np
from jax import lax
from jax.experimental import pallas as pl
from jax.experimental.pallas import tpu as pltpu
from jax.sharding import PartitionSpec as P

MESH = pl.DeviceIdType.MESH
C = 32
K = 3
PZ = 4
PY = 8
X = 128
MAXP = 4
M = 4
f32 = jnp.float32
bf16 = jnp.bfloat16


def bell(length):
    position = np.arange(length, dtype=np.float64)
    center = (length - 1) / 2.0
    sigma = length / 4.0
    return [float(v) for v in np.exp(-((position - center) ** 2) / (2.0 * sigma * sigma))]


def bell_x(shape):
    position = lax.broadcasted_iota(jnp.int32, shape, len(shape) - 1).astype(f32)
    center = (X - 1) / 2.0
    sigma = X / 4.0
    return jnp.exp(-((position - center) ** 2) / (2.0 * sigma * sigma))


def picked(values, index):
    out = jnp.full(index.shape, values[0], f32)
    for i in range(1, len(values)):
        out = jnp.where(index == i, f32(values[i]), out)
    return out


def kernel(
    depth, slabs,
    feat, cz_ref, cy_ref, cnt_ref, w_ref, gain_ref, shift_ref, segw_ref, segb_ref,
    out_ref,
    featv, staged, own, ints, ints_in, sendp, recvp, wall, prm, wa, wb, w9, seg, im, im9, hid,
    sums, tsend, tin, tback, pad_in, pad_own, gpad, inv,
    feat_sem, int_s, int_r, pl_s, pl_r, w_s, w_r, p_s, p_r, a_s, a_r, b_s, b_r, c_s, c_r,
):
    m = lax.axis_index("member")
    v = lax.axis_index("vol")
    nxt = lax.rem(v + 1, slabs)
    prv = lax.rem(v + slabs - 1, slabs)
    mates = [lax.rem(m + d, M) for d in range(1, M)]
    froms = [lax.rem(m + M - d, M) for d in range(1, M)]
    rows = featv.shape[2]

    feat_copy = pltpu.make_async_copy(feat, featv, feat_sem)
    feat_copy.start()

    barrier = pltpu.get_barrier_semaphore()
    for target in [(m, nxt), (m, prv)] + [(mate, v) for mate in mates]:
        pl.semaphore_signal(barrier, inc=1, device_id=target, device_id_type=MESH)

    lane = lax.broadcasted_iota(jnp.int32, (8, X), 1)
    row = jnp.where(lane == 8, cnt_ref[0], 0)
    for k in range(MAXP):
        row = jnp.where(lane == k, cz_ref[0, k], row)
        row = jnp.where(lane == 4 + k, cy_ref[0, k], row)
    ints[...] = row

    for kz in range(3):
        for ky in range(3):
            for kx in range(3):
                from_y = jnp.where((m // 2) % 2 == 1, 2 - ky, ky)
                from_x = jnp.where(m % 2 == 1, 2 - kx, kx)
                tap = w_ref[kz, from_y, from_x]
                t = ky * 3 + kx
                at = kz * 256 + t * C if t < 8 else 768 + kz * C
                wall[m, :, at:at + C] = tap
    prm[m] = jnp.zeros((8, X), f32)
    prm[m, 0:1, 0:C] = gain_ref[...]
    prm[m, 1:2, 0:C] = shift_ref[...]
    prm[m, 2:5, 0:C] = segw_ref[0].astype(f32)
    prm[m, 5:6, 0:K] = segb_ref[...]

    pl.semaphore_wait(barrier, 2 + len(mates))

    int_copy = pltpu.make_async_remote_copy(
        src_ref=ints, dst_ref=ints_in, send_sem=int_s, recv_sem=int_r,
        device_id=(m, nxt), device_id_type=MESH)
    int_copy.start()

    def shared(buf, send, recv, d):
        return pltpu.make_async_remote_copy(
            src_ref=buf.at[m], dst_ref=buf.at[m], send_sem=send.at[d], recv_sem=recv.at[d],
            device_id=(mates[d], v), device_id_type=MESH)

    def arrives(buf, send, recv, d):
        return pltpu.make_async_remote_copy(
            src_ref=buf.at[froms[d]], dst_ref=buf.at[froms[d]], send_sem=send.at[d], recv_sem=recv.at[d],
            device_id=(mates[d], v), device_id_type=MESH)

    for d in range(M - 1):
        shared(wall, w_s, w_r, d).start()
        shared(prm, p_s, p_r, d).start()

    def chosen(ref_row):
        value = ref_row(0)
        for k in range(1, MAXP):
            value = jnp.where(m == k, ref_row(k), value)
        return value

    my_z = chosen(lambda k: cz_ref[0, k])
    my_y = chosen(lambda k: cy_ref[0, k])
    feat_copy.wait()

    def plane_copy(j):
        return pltpu.make_async_remote_copy(
            src_ref=sendp.at[j], dst_ref=recvp.at[j], send_sem=pl_s.at[j], recv_sem=pl_r.at[j],
            device_id=(m, nxt), device_id_type=MESH)

    for j in range(PZ):
        z = jnp.minimum(my_z + j, depth - 1)

        def stage(c, carry, z=z):
            staged[pl.ds(c * rows, rows), :] = featv[c, z].astype(f32)
            return carry

        lax.fori_loop(0, C, stage, 0, unroll=8)

        def pick(y, carry, j=j):
            sendp[j, y] = staged[pl.ds(my_y + y, C, stride=rows), :].astype(bf16)
            return carry

        lax.fori_loop(0, PY, pick, 0, unroll=4)
        plane_copy(j).start()

    inside = (v > 0).astype(f32)
    for j in range(PZ - 1):
        def stage(c, carry, j=j):
            own[pl.ds(j * C * rows + c * rows, rows), :] = featv[c, j].astype(f32) * inside
            return carry

        lax.fori_loop(0, C, stage, 0, unroll=8)

    for j in range(PZ):
        for kx in range(3):
            im[j * 256 + kx * C:j * 256 + (kx + 1) * C, X:2 * X] = jnp.zeros((C, X), bf16)
        for kx in range(2):
            t = 6 + kx
            im[j * 256 + t * C:j * 256 + (t + 1) * C, 8 * X:9 * X] = jnp.zeros((C, X), bf16)
        im9[j * C:(j + 1) * C, 8 * X:9 * X] = jnp.zeros((C, X), bf16)

    int_copy.wait_recv()
    got = ints_in[...]
    prev_z = [jnp.sum(jnp.where(lane[0:1] == k, got[0:1], 0)) for k in range(MAXP)]
    prev_y = [jnp.sum(jnp.where(lane[0:1] == 4 + k, got[0:1], 0)) for k in range(MAXP)]
    prev_count = jnp.sum(jnp.where(lane[0:1] == 8, got[0:1], 0))
    at_z = chosen(lambda k: prev_z[k])
    at_y = chosen(lambda k: prev_y[k])

    gz, gy = bell(PZ), bell(PY)
    gyx = picked(gy, lax.broadcasted_iota(jnp.int32, (PY, X), 0)) * bell_x((PY, X))
    nothing = jnp.zeros((PY, X), f32)
    for j in range(PZ + 2):
        gpad[j, 0:8] = nothing
        gpad[j, 16:24] = nothing
        gpad[j, 8:16] = nothing if j in (0, PZ + 1) else gyx * (gz[j - 1] * M)
    for pad in (pad_in, pad_own):
        for s in range(MAXP):
            for j in range(PZ + 2):
                for k in range(K - 1):
                    pad[s, j, k, 0:8] = nothing
                    pad[s, j, k, 16:24] = nothing
                    if j in (0, PZ + 1):
                        pad[s, j, k, 8:16] = nothing

    first = m * PY
    own_off = [8 + jnp.clip(first - cy_ref[0, k], -8, 8) for k in range(MAXP)]
    in_off = [8 + jnp.clip(first - prev_y[k], -8, 8) for k in range(MAXP)]
    own_live = [(k < cnt_ref[0]).astype(f32) for k in range(MAXP)]
    in_live = [((k < prev_count) & (v > 0)).astype(f32) for k in range(MAXP)]

    def which(z):
        return 1 + jnp.clip(z, -1, PZ)

    def weigh(z, carry):
        total = jnp.zeros((PY, X), f32)
        for k in range(MAXP):
            total = total + gpad[which(z - cz_ref[0, k]), pl.ds(own_off[k], 8), :] * own_live[k]
            total = total + gpad[which(z + depth - prev_z[k]), pl.ds(in_off[k], 8), :] * in_live[k]
        inv[z] = 1.0 / jnp.maximum(total, 0.1)
        return carry

    lax.fori_loop(0, depth, weigh, 0)

    for d in range(M - 1):
        arrives(wall, w_s, w_r, d).wait_recv()
        arrives(prm, p_s, p_r, d).wait_recv()
    wa[...] = jnp.zeros(wa.shape, bf16)
    wb[...] = jnp.zeros(wb.shape, bf16)
    w9[...] = jnp.zeros(w9.shape, bf16)
    for q in range(M):
        r = q * C
        full = wall[q, :, 0:768]
        wa[r:r + C, 0:512] = full[:, 256:768]
        wa[128 + r:128 + r + C, :] = full
        wb[r:r + C, :] = full
        wb[128 + r:128 + r + C, 256:768] = full[:, 0:512]
        for o in range(PZ):
            for kz in range(3):
                j = o + kz - 1
                if 0 <= j < PZ:
                    w9[o * 128 + r:o * 128 + r + C, j * C:(j + 1) * C] = wall[q, :, 768 + kz * C:768 + (kz + 1) * C]

    def column(values):
        eye = lax.broadcasted_iota(jnp.int32, (C, C), 0) == lax.broadcasted_iota(jnp.int32, (C, C), 1)
        return jnp.sum(jnp.where(eye, jnp.broadcast_to(values, (C, C)), 0.0), axis=1, keepdims=True)

    gain = jnp.concatenate([column(prm[q, 0:1, 0:C]) for q in range(M)], axis=0)
    shift = jnp.concatenate([column(prm[q, 1:2, 0:C]) for q in range(M)], axis=0)
    seg[...] = jnp.zeros(seg.shape, f32)
    for q in range(M):
        for o in range(2):
            at = o * 128 + q * C
            for k in range(K - 1):
                seg[k * 2 + o:k * 2 + o + 1, at:at + C] = prm[q, 2 + k:3 + k, 0:C]
                seg[8 + k * 2 + o:8 + k * 2 + o + 1, at:at + C] = prm[q, 4:5, 0:C]
    head = seg[...].astype(bf16)
    offsets = prm[0, 5:6, :] + prm[1, 5:6, :] + prm[2, 5:6, :] + prm[3, 5:6, :]
    offset = [jnp.sum(jnp.where(lane[0:1] == k, offsets, 0.0)) for k in range(K)]
    sub = lax.broadcasted_iota(jnp.int32, (8, 1), 0)
    bias = jnp.where(sub < 2, offset[0] - offset[2], offset[1] - offset[2])

    lane_row = lax.broadcasted_iota(jnp.int32, (C, X), 1)
    for j in range(PZ):
        plane_copy(j).wait_recv()
        beyond = at_z + j - depth
        start = jnp.clip(beyond, 0, PZ - 2) * (C * rows) + at_y

        def expand(y, carry, j=j, beyond=beyond, start=start):
            value = recvp[j, y].astype(f32)
            if j > 0:
                value = jnp.where(beyond >= 0, own[pl.ds(start + y, C, stride=rows), :], value)
            left = jnp.where(lane_row == 0, 0.0, pltpu.roll(value, 1, 1)).astype(bf16)
            right = jnp.where(lane_row == X - 1, 0.0, pltpu.roll(value, X - 1, 1)).astype(bf16)
            middle = value.astype(bf16)
            for ky in range(3):
                at = pl.ds(pl.multiple_of((y - ky + 2) * X, X), X)
                for kx, part in enumerate((left, middle, right)):
                    t = ky * 3 + kx
                    if t < 8:
                        im[j * 256 + t * C:j * 256 + (t + 1) * C, at] = part
                    else:
                        im9[j * C:(j + 1) * C, at] = part
            return carry

        lax.fori_loop(0, PY, expand, 0, unroll=2)

    sums[...] = jnp.zeros(sums.shape, f32)
    for p, taps in enumerate((wa, wb)):
        def conv(n, carry, p=p, taps=taps):
            at = pl.ds(pl.multiple_of(X + n * 256, X), 256)
            got = jnp.dot(taps[...], im[p * 256:p * 256 + 768, at], preferred_element_type=f32)
            got = got + jnp.dot(w9[p * 256:(p + 1) * 256, :], im9[:, at], preferred_element_type=f32)
            hid[p, :, pl.ds(pl.multiple_of(n * 256, 256), 256)] = got
            pair = got[:128] + got[128:]
            sums[...] += pair[:, :X] + pair[:, X:]
            return carry

        lax.fori_loop(0, 4, conv, 0)

    voxels = PZ * PY * X
    mean = jnp.sum(sums[...], axis=1, keepdims=True) / voxels
    sums[...] = jnp.zeros(sums.shape, f32)
    for p in range(2):
        def spread(n, carry, p=p):
            got = hid[p, :, pl.ds(pl.multiple_of(n * 256, 256), 256)]
            low = got[:128] - mean
            high = got[128:] - mean
            pair = low * low + high * high
            sums[...] += pair[:, :X] + pair[:, X:]
            return carry

        lax.fori_loop(0, 4, spread, 0)
    variance = jnp.sum(sums[...], axis=1, keepdims=True) / voxels
    scale = lax.rsqrt(variance + 1e-05) * gain

    alive = m < prev_count
    gx = bell_x((8, X))
    for p in range(2):
        gzp = jnp.where(sub % 2 == 0, f32(gz[2 * p]), f32(gz[2 * p + 1]))

        def classify(n, carry, p=p, gzp=gzp):
            parts = []
            for o in range(2):
                got = hid[p, o * 128:(o + 1) * 128, pl.ds(pl.multiple_of(n * 256, 256), 256)]
                normed = (got - mean) * scale + shift
                parts.append(jnp.maximum(normed, 0.01 * normed).astype(bf16))
            act = jnp.concatenate(parts, axis=0)
            both = jnp.dot(head, act, preferred_element_type=f32)
            logit = both[0:8] - both[8:16] + bias
            for h in range(2):
                y = n * 2 + h
                gyv = f32(gy[0])
                for i in range(1, PY):
                    gyv = jnp.where(y == i, f32(gy[i]), gyv)
                value = logit[:, h * X:(h + 1) * X] * (gx * gzp * gyv)
                value = jnp.where(alive, value, 0.0)
                tsend[p, pl.ds(y, 8, stride=8), :] = value
            return carry

        lax.fori_loop(0, 4, classify, 0)

    back = pltpu.make_async_remote_copy(
        src_ref=tsend.at[:, pl.ds(0, 32)], dst_ref=tback.at[m], send_sem=b_s, recv_sem=b_r,
        device_id=(m, prv), device_id_type=MESH)
    back.start()

    def across(d):
        return pltpu.make_async_remote_copy(
            src_ref=tsend.at[:, pl.ds(0, 32)], dst_ref=tin.at[m], send_sem=a_s.at[d], recv_sem=a_r.at[d],
            device_id=(mates[d], v), device_id_type=MESH)

    for d in range(M - 1):
        across(d).start()
    back.wait_recv()
    for d in range(M - 1):
        shared(tback, c_s, c_r, d).start()
    tin[m] = tsend[:, 0:32]

    def spread_out(buf, pad, s):
        for p in range(2):
            for k in range(K - 1):
                for o in range(2):
                    r = (k * 2 + o) * 8
                    pad[s, 1 + 2 * p + o, k, 8:16] = buf[s, p, r:r + 8]

    for d in range(M - 1):
        arrives(tin, a_s, a_r, d).wait_recv()
    for s in range(MAXP):
        spread_out(tin, pad_in, s)
    for d in range(M - 1):
        arrives(tback, c_s, c_r, d).wait_recv()
    for s in range(MAXP):
        spread_out(tback, pad_own, s)

    def finish(z, spill):
        diff = []
        for k in range(K - 1):
            total = jnp.zeros((PY, X), f32)
            for s in range(MAXP):
                total = total + pad_own[s, which(z - cz_ref[0, s]), k, pl.ds(own_off[s], 8), :]
                if spill:
                    total = total + pad_in[s, which(z + depth - prev_z[s]), k, pl.ds(in_off[s], 8), :] * inside
            diff.append(total * inv[z])
        top = jnp.maximum(jnp.maximum(diff[0], diff[1]), 0.0)
        powers = [jnp.exp(diff[0] - top), jnp.exp(diff[1] - top), jnp.exp(-top)]
        whole = 1.0 / (powers[0] + powers[1] + powers[2])
        for k in range(K):
            out_ref[k, z] = powers[k] * whole

    for z in range(PZ - 1):
        finish(z, True)

    def rest(z, carry):
        finish(z, False)
        return carry

    lax.fori_loop(PZ - 1, depth, rest, 0)

    int_copy.wait_send()
    for j in range(PZ):
        plane_copy(j).wait_send()
    back.wait_send()
    for d in range(M - 1):
        shared(wall, w_s, w_r, d).wait_send()
        shared(prm, p_s, p_r, d).wait_send()
        across(d).wait_send()
        shared(tback, c_s, c_r, d).wait_send()


def per_device(slabs, features, corner_z, corner_y, counts, conv_w, norm_gain, norm_shift, seg_w, seg_b):
    channels, depth, rows, width = features.shape
    taps = conv_w[0].transpose(2, 3, 4, 0, 1)
    smem = pl.BlockSpec(memory_space=pltpu.SMEM)
    vmem = pl.BlockSpec(memory_space=pltpu.VMEM)
    dma = pltpu.SemaphoreType.DMA
    return pl.pallas_call(
        functools.partial(kernel, depth, slabs),
        name="ensemble_patches",
        out_shape=jax.ShapeDtypeStruct((K, depth, rows // M, width), f32),
        in_specs=[pl.BlockSpec(memory_space=pl.ANY), smem, smem, smem] + [vmem] * 5,
        out_specs=vmem,
        scratch_shapes=[
            pltpu.VMEM((channels, depth, rows, width), bf16),
            pltpu.VMEM((C * rows, X), f32),
            pltpu.VMEM(((PZ - 1) * C * rows, X), f32),
            pltpu.VMEM((8, X), jnp.int32),
            pltpu.VMEM((8, X), jnp.int32),
            pltpu.VMEM((PZ, PY, C, X), bf16),
            pltpu.VMEM((PZ, PY, C, X), bf16),
            pltpu.VMEM((M, C, 896), bf16),
            pltpu.VMEM((M, 8, X), f32),
            pltpu.VMEM((256, 768), bf16),
            pltpu.VMEM((256, 768), bf16),
            pltpu.VMEM((512, 128), bf16),
            pltpu.VMEM((16, 256), f32),
            pltpu.VMEM((PZ * 256, 10 * X), bf16),
            pltpu.VMEM((PZ * C, 10 * X), bf16),
            pltpu.VMEM((2, 256, PY * X), f32),
            pltpu.VMEM((128, X), f32),
            pltpu.VMEM((2, 64, X), f32),
            pltpu.VMEM((M, 2, 32, X), f32),
            pltpu.VMEM((M, 2, 32, X), f32),
            pltpu.VMEM((MAXP, PZ + 2, K - 1, 24, X), f32),
            pltpu.VMEM((MAXP, PZ + 2, K - 1, 24, X), f32),
            pltpu.VMEM((PZ + 2, 24, X), f32),
            pltpu.VMEM((depth, PY, X), f32),
            dma, dma, dma, dma((PZ,)), dma((PZ,)), dma((3,)), dma((3,)), dma((3,)), dma((3,)),
            dma((3,)), dma((3,)), dma, dma, dma((3,)), dma((3,)),
        ],
        compiler_params=pltpu.CompilerParams(
            collective_id=0, has_side_effects=True, vmem_limit_bytes=40 * 1024 * 1024),
    )(features, corner_z, corner_y, counts, taps, norm_gain, norm_shift, seg_w, seg_b)


def solution(mesh):
    placed = (
        P(None, "vol", None, None),
        P("vol", None),
        P("vol", None),
        P("vol"),
        P("member", None, None, None, None, None),
        P("member", None),
        P("member", None),
        P("member", None, None),
        P("member", None),
    )
    return jax.shard_map(
        functools.partial(per_device, mesh.shape["vol"]),
        mesh=mesh,
        in_specs=placed,
        out_specs=P(None, "vol", "member", None),
        check_vma=False,
    )
```

profile of v0, /device:TPU:2, one launch (start us, length us, event | category | flops | bytes accessed | tf_op | source)
XLA Modules:
  0.0 33.6 jit_solution(4757951820921419021)
XLA Ops:
  0.7 0.0 copy-start
  0.7 2.2 %copy-done = bf16[32,16,32,128]{3,2,1,0:T(8,128)(2,1)S(1)} copy-done((bf16[32,16,32,128]{3,2,1,0:T(8,128)(2,1)S(1)}, bf16[32,16,32,128]{3,2,1,0:T(8,128)(2,1)}, u32[]{:S(2)}) %copy-start) | copy-done | bytes 4194328
  2.8 0.0 copy-start.1
  2.8 0.9 %copy-done.1 = bf16[1,32,32,3,3,3]{2,1,5,4,3,0:T(8,128)(2,1)S(1)} copy-done((bf16[1,32,32,3,3,3]{2,1,5,4,3,0:T(8,128)(2,1)S(1)}, bf16[1,32,32,3,3,3]{2,1,5,4,3,0:T(8,128)(2,1)}, u32[]{:S(2)}) %copy-start.1) | copy-done | bytes 55320
  3.8 0.0 copy-start.2
  3.8 0.7 %copy-done.2 = bf16[1,3,32]{2,1,0:T(4,128)(2,1)S(1)} copy-done((bf16[1,3,32]{2,1,0:T(4,128)(2,1)S(1)}, bf16[1,3,32]{2,1,0:T(4,128)(2,1)}, u32[]{:S(2)}) %copy-start.2) | copy-done | bytes 216
  4.5 0.0 copy-start.3
  4.5 0.7 %copy-done.3 = s32[1,4]{1,0:T(1,128)S(1)} copy-done((s32[1,4]{1,0:T(1,128)S(1)}, s32[1,4]{1,0:T(1,128)}, u32[]{:S(2)}) %copy-start.3) | copy-done | bytes 40
  5.1 0.0 copy-start.4
  5.1 0.7 %copy-done.4 = s32[1,4]{1,0:T(1,128)S(1)} copy-done((s32[1,4]{1,0:T(1,128)S(1)}, s32[1,4]{1,0:T(1,128)}, u32[]{:S(2)}) %copy-start.4) | copy-done | bytes 40
  5.8 0.0 copy-start.5
  5.8 0.7 %copy-done.5 = f32[1,32]{1,0:T(1,128)S(1)} copy-done((f32[1,32]{1,0:T(1,128)S(1)}, f32[1,32]{1,0:T(1,128)}, u32[]{:S(2)}) %copy-start.5) | copy-done | bytes 152
  6.4 0.0 copy-start.6
  6.4 0.7 %copy-done.6 = f32[1,32]{1,0:T(1,128)S(1)} copy-done((f32[1,32]{1,0:T(1,128)S(1)}, f32[1,32]{1,0:T(1,128)}, u32[]{:S(2)}) %copy-start.6) | copy-done | bytes 152
  7.1 0.0 copy-start.7
  7.1 0.7 %copy-done.7 = f32[1,3]{1,0:T(1,128)S(1)} copy-done((f32[1,3]{1,0:T(1,128)S(1)}, f32[1,3]{1,0:T(1,128)}, u32[]{:S(2)}) %copy-start.7) | copy-done | bytes 36
  7.7 25.2 %ensemble_patches.1 = f32[3,16,8,128]{3,2,1,0:T(8,128)S(1)} custom-call(bf16[32,16,32,128]{3,2,1,0:T(8,128)(2,1)S(1)} %copy-done, s32[1,4]{1,0:T(1,128)S(1)} %copy-done.3, s32[1,4]{1,0:T(1,128)S(1)} %copy-done.4, s32[1]{0:T(128)S(6)} %copy.11.cnt_ref, bf16[3,3,3,32,32]{4,3,2,1,0:T(8,128)(2,1)S(1)} %bitcast.3, f32[1,32]{1,0:T(1,128)S(1)} %copy-done.5, ...), custom_call_target="tpu_custom_call" | custom-call | tf_op jit(solution)/shard_map/ensemble_patches/pallas_call | solution.py:392
  32.9 0.7 %copy.12 = f32[3,16,8,128]{3,2,1,0:T(8,128)} copy(f32[3,16,8,128]{3,2,1,0:T(8,128)S(1)} %ensemble_patches.1) | data formatting | bytes 393216
Async XLA Ops:
  0.7 2.2 %copy-start = (bf16[32,16,32,128]{3,2,1,0:T(8,128)(2,1)S(1)}, bf16[32,16,32,128]{3,2,1,0:T(8,128)(2,1)}, u32[]{:S(2)}) copy-start(bf16[32,16,32,128]{3,2,1,0:T(8,128)(2,1)} %feat.1) | copy-start | bytes 12582916
  2.8 0.9 %copy-start.1 = (bf16[1,32,32,3,3,3]{2,1,5,4,3,0:T(8,128)(2,1)S(1)}, bf16[1,32,32,3,3,3]{2,1,5,4,3,0:T(8,128)(2,1)}, u32[]{:S(2)}) copy-start(bf16[1,32,32,3,3,3]{2,1,5,4,3,0:T(8,128)(2,1)} %param.13) | copy-start | bytes 165892
  3.8 0.7 %copy-start.2 = (bf16[1,3,32]{2,1,0:T(4,128)(2,1)S(1)}, bf16[1,3,32]{2,1,0:T(4,128)(2,1)}, u32[]{:S(2)}) copy-start(bf16[1,3,32]{2,1,0:T(4,128)(2,1)} %segw_ref.1) | copy-start | bytes 580
  4.5 0.7 %copy-start.3 = (s32[1,4]{1,0:T(1,128)S(1)}, s32[1,4]{1,0:T(1,128)}, u32[]{:S(2)}) copy-start(s32[1,4]{1,0:T(1,128)} %cz_ref.1) | copy-start | bytes 52
  5.1 0.7 %copy-start.4 = (s32[1,4]{1,0:T(1,128)S(1)}, s32[1,4]{1,0:T(1,128)}, u32[]{:S(2)}) copy-start(s32[1,4]{1,0:T(1,128)} %cy_ref.1) | copy-start | bytes 52
  5.8 0.7 %copy-start.5 = (f32[1,32]{1,0:T(1,128)S(1)}, f32[1,32]{1,0:T(1,128)}, u32[]{:S(2)}) copy-start(f32[1,32]{1,0:T(1,128)} %gain_ref.1) | copy-start | bytes 388
  6.4 0.7 %copy-start.6 = (f32[1,32]{1,0:T(1,128)S(1)}, f32[1,32]{1,0:T(1,128)}, u32[]{:S(2)}) copy-start(f32[1,32]{1,0:T(1,128)} %shift_ref.1) | copy-start | bytes 388
  7.1 0.7 %copy-start.7 = (f32[1,3]{1,0:T(1,128)S(1)}, f32[1,3]{1,0:T(1,128)}, u32[]{:S(2)}) copy-start(f32[1,3]{1,0:T(1,128)} %segb_ref.1) | copy-start | bytes 40
where the time goes:
time: 34.1 us; the launch traced here: 33.6 us
  Pallas kernels  25.2 us (74%)
  local copies, waits for them, and re-layouts  7.75 us (23%)
  between operations  0.68 us (2%)
    pallas_call x1, Pallas kernels, per_device(): pl.pallas_call(functools.partial(kernel, depth, slabs), name='ensemble_pa...  25.2 us
    unnamed x17, local copies, waits for them, and re-layouts  7.75 us

commit v1 on v0

--- a/solution.py
+++ b/solution.py
@@ -43,11 +43,11 @@
 
 def kernel(
     depth, slabs,
-    feat, cz_ref, cy_ref, cnt_ref, w_ref, gain_ref, shift_ref, segw_ref, segb_ref,
+    feat, cz_hbm, cy_hbm, cnt_hbm, w_hbm, gain_hbm, shift_hbm, segw_hbm, segb_hbm,
     out_ref,
-    featv, staged, own, ints, ints_in, sendp, recvp, wall, prm, wa, wb, w9, seg, im, im9, hid,
+    cz_ref, cy_ref, cnt_ref, w_ref, gain_ref, shift_ref, segw_ref, segb_ref, featv, staged, own, ints, ints_in, sendp, recvp, wall, prm, wa, wb, w9, seg, im, im9, hid,
     sums, tsend, tin, tback, pad_in, pad_own, gpad, inv,
-    feat_sem, int_s, int_r, pl_s, pl_r, w_s, w_r, p_s, p_r, a_s, a_r, b_s, b_r, c_s, c_r,
+    small_sem, feat_sem, int_s, int_r, pl_s, pl_r, w_s, w_r, p_s, p_r, a_s, a_r, b_s, b_r, c_s, c_r,
 ):
     m = lax.axis_index("member")
     v = lax.axis_index("vol")
@@ -57,12 +57,23 @@
     froms = [lax.rem(m + M - d, M) for d in range(1, M)]
     rows = featv.shape[2]
 
+    small = [
+        pltpu.make_async_copy(src, dst, small_sem.at[i])
+        for i, (src, dst) in enumerate((
+            (cz_hbm, cz_ref), (cy_hbm, cy_ref), (cnt_hbm, cnt_ref), (w_hbm, w_ref), (gain_hbm, gain_ref),
+            (shift_hbm, shift_ref), (segw_hbm, segw_ref), (segb_hbm, segb_ref)))
+    ]
+    for copy in small:
+        copy.start()
     feat_copy = pltpu.make_async_copy(feat, featv, feat_sem)
     feat_copy.start()
 
     barrier = pltpu.get_barrier_semaphore()
     for target in [(m, nxt), (m, prv)] + [(mate, v) for mate in mates]:
         pl.semaphore_signal(barrier, inc=1, device_id=target, device_id_type=MESH)
+
+    for copy in small:
+        copy.wait()
 
     lane = lax.broadcasted_iota(jnp.int32, (8, X), 1)
     row = jnp.where(lane == 8, cnt_ref[0], 0)
@@ -386,16 +397,22 @@
 def per_device(slabs, features, corner_z, corner_y, counts, conv_w, norm_gain, norm_shift, seg_w, seg_b):
     channels, depth, rows, width = features.shape
     taps = conv_w[0].transpose(2, 3, 4, 0, 1)
-    smem = pl.BlockSpec(memory_space=pltpu.SMEM)
-    vmem = pl.BlockSpec(memory_space=pltpu.VMEM)
     dma = pltpu.SemaphoreType.DMA
     return pl.pallas_call(
         functools.partial(kernel, depth, slabs),
         name="ensemble_patches",
         out_shape=jax.ShapeDtypeStruct((K, depth, rows // M, width), f32),
-        in_specs=[pl.BlockSpec(memory_space=pl.ANY), smem, smem, smem] + [vmem] * 5,
-        out_specs=vmem,
+        in_specs=[pl.BlockSpec(memory_space=pltpu.HBM)] * 9,
+        out_specs=pl.BlockSpec(memory_space=pltpu.VMEM),
         scratch_shapes=[
+            pltpu.SMEM((1, MAXP), jnp.int32),
+            pltpu.SMEM((1, MAXP), jnp.int32),
+            pltpu.SMEM((1,), jnp.int32),
+            pltpu.VMEM((3, 3, 3, C, C), bf16),
+            pltpu.VMEM((1, C), f32),
+            pltpu.VMEM((1, C), f32),
+            pltpu.VMEM((1, K, C), bf16),
+            pltpu.VMEM((1, K), f32),
             pltpu.VMEM((channels, depth, rows, width), bf16),
             pltpu.VMEM((C * rows, X), f32),
             pltpu.VMEM(((PZ - 1) * C * rows, X), f32),
@@ -420,7 +437,7 @@
             pltpu.VMEM((MAXP, PZ + 2, K - 1, 24, X), f32),
             pltpu.VMEM((PZ + 2, 24, X), f32),
             pltpu.VMEM((depth, PY, X), f32),
-            dma, dma, dma, dma((PZ,)), dma((PZ,)), dma((3,)), dma((3,)), dma((3,)), dma((3,)),
+            dma((8,)), dma, dma, dma, dma((PZ,)), dma((PZ,)), dma((3,)), dma((3,)), dma((3,)), dma((3,)),
             dma((3,)), dma((3,)), dma, dma, dma((3,)), dma((3,)),
         ],
         compiler_params=pltpu.CompilerParams(

time: 34.1 us -> 33.9 us (level)
  no operation moved by 1% of the time
where the time goes in v1:
time: 33.9 us; the launch traced here: 33.4 us
  Pallas kernels  25 us (74%)
  local copies, waits for them, and re-layouts  7.75 us (23%)
  between operations  0.68 us (2%)
    pallas_call x1, Pallas kernels, per_device(): pl.pallas_call(functools.partial(kernel, depth, slabs), name='ensemble_pa...  25 us
    unnamed x17, local copies, waits for them, and re-layouts  7.75 us

profile of v1, /device:TPU:2, one launch (start us, length us, event | category | flops | bytes accessed | tf_op | source)
XLA Modules:
  0.0 33.4 jit_solution(9544827748844876952)
XLA Ops:
  0.7 0.0 copy-start
  0.7 2.2 %copy-done = bf16[32,16,32,128]{3,2,1,0:T(8,128)(2,1)S(1)} copy-done((bf16[32,16,32,128]{3,2,1,0:T(8,128)(2,1)S(1)}, bf16[32,16,32,128]{3,2,1,0:T(8,128)(2,1)}, u32[]{:S(2)}) %copy-start) | copy-done | bytes 4194328
  2.8 0.0 copy-start.1
  2.8 0.9 %copy-done.1 = bf16[1,32,32,3,3,3]{2,1,5,4,3,0:T(8,128)(2,1)S(1)} copy-done((bf16[1,32,32,3,3,3]{2,1,5,4,3,0:T(8,128)(2,1)S(1)}, bf16[1,32,32,3,3,3]{2,1,5,4,3,0:T(8,128)(2,1)}, u32[]{:S(2)}) %copy-start.1) | copy-done | bytes 55320
  3.8 0.0 copy-start.2
  3.8 0.7 %copy-done.2 = bf16[1,3,32]{2,1,0:T(4,128)(2,1)S(1)} copy-done((bf16[1,3,32]{2,1,0:T(4,128)(2,1)S(1)}, bf16[1,3,32]{2,1,0:T(4,128)(2,1)}, u32[]{:S(2)}) %copy-start.2) | copy-done | bytes 216
  4.5 0.0 copy-start.3
  4.5 0.7 %copy-done.3 = s32[1,4]{1,0:T(1,128)S(1)} copy-done((s32[1,4]{1,0:T(1,128)S(1)}, s32[1,4]{1,0:T(1,128)}, u32[]{:S(2)}) %copy-start.3) | copy-done | bytes 40
  5.1 0.0 copy-start.4
  5.1 0.7 %copy-done.4 = s32[1,4]{1,0:T(1,128)S(1)} copy-done((s32[1,4]{1,0:T(1,128)S(1)}, s32[1,4]{1,0:T(1,128)}, u32[]{:S(2)}) %copy-start.4) | copy-done | bytes 40
  5.8 0.0 copy-start.5
  5.8 0.7 %copy-done.5 = f32[1,32]{1,0:T(1,128)S(1)} copy-done((f32[1,32]{1,0:T(1,128)S(1)}, f32[1,32]{1,0:T(1,128)}, u32[]{:S(2)}) %copy-start.5) | copy-done | bytes 152
  6.4 0.0 copy-start.6
  6.4 0.7 %copy-done.6 = f32[1,32]{1,0:T(1,128)S(1)} copy-done((f32[1,32]{1,0:T(1,128)S(1)}, f32[1,32]{1,0:T(1,128)}, u32[]{:S(2)}) %copy-start.6) | copy-done | bytes 152
  7.1 0.0 copy-start.7
  7.1 0.7 %copy-done.7 = f32[1,3]{1,0:T(1,128)S(1)} copy-done((f32[1,3]{1,0:T(1,128)S(1)}, f32[1,3]{1,0:T(1,128)}, u32[]{:S(2)}) %copy-start.7) | copy-done | bytes 36
  7.7 25.0 %ensemble_patches.1 = f32[3,16,8,128]{3,2,1,0:T(8,128)S(1)} custom-call(bf16[32,16,32,128]{3,2,1,0:T(8,128)(2,1)S(1)} %copy-done, s32[1,4]{1,0:T(1,128)S(1)} %copy-done.3, s32[1,4]{1,0:T(1,128)S(1)} %copy-done.4, s32[1]{0:T(128)S(6)} %copy.11.cnt_hbm, bf16[3,3,3,32,32]{4,3,2,1,0:T(8,128)(2,1)S(1)} %bitcast.3, f32[1,32]{1,0:T(1,128)S(1)} %copy-done.5, ...), custom_call_target="tpu_custom_call" | custom-call | tf_op jit(solution)/shard_map/ensemble_patches/pallas_call | solution.py:401
  32.7 0.7 %copy.12 = f32[3,16,8,128]{3,2,1,0:T(8,128)} copy(f32[3,16,8,128]{3,2,1,0:T(8,128)S(1)} %ensemble_patches.1) | data formatting | bytes 393216
Async XLA Ops:
  0.7 2.2 %copy-start = (bf16[32,16,32,128]{3,2,1,0:T(8,128)(2,1)S(1)}, bf16[32,16,32,128]{3,2,1,0:T(8,128)(2,1)}, u32[]{:S(2)}) copy-start(bf16[32,16,32,128]{3,2,1,0:T(8,128)(2,1)} %feat.1) | copy-start | bytes 12582916
  2.8 0.9 %copy-start.1 = (bf16[1,32,32,3,3,3]{2,1,5,4,3,0:T(8,128)(2,1)S(1)}, bf16[1,32,32,3,3,3]{2,1,5,4,3,0:T(8,128)(2,1)}, u32[]{:S(2)}) copy-start(bf16[1,32,32,3,3,3]{2,1,5,4,3,0:T(8,128)(2,1)} %param.13) | copy-start | bytes 165892
  3.8 0.7 %copy-start.2 = (bf16[1,3,32]{2,1,0:T(4,128)(2,1)S(1)}, bf16[1,3,32]{2,1,0:T(4,128)(2,1)}, u32[]{:S(2)}) copy-start(bf16[1,3,32]{2,1,0:T(4,128)(2,1)} %segw_hbm.1) | copy-start | bytes 580
  4.5 0.7 %copy-start.3 = (s32[1,4]{1,0:T(1,128)S(1)}, s32[1,4]{1,0:T(1,128)}, u32[]{:S(2)}) copy-start(s32[1,4]{1,0:T(1,128)} %cz_hbm.1) | copy-start | bytes 52
  5.1 0.7 %copy-start.4 = (s32[1,4]{1,0:T(1,128)S(1)}, s32[1,4]{1,0:T(1,128)}, u32[]{:S(2)}) copy-start(s32[1,4]{1,0:T(1,128)} %cy_hbm.1) | copy-start | bytes 52
  5.8 0.7 %copy-start.5 = (f32[1,32]{1,0:T(1,128)S(1)}, f32[1,32]{1,0:T(1,128)}, u32[]{:S(2)}) copy-start(f32[1,32]{1,0:T(1,128)} %gain_hbm.1) | copy-start | bytes 388
  6.4 0.7 %copy-start.6 = (f32[1,32]{1,0:T(1,128)S(1)}, f32[1,32]{1,0:T(1,128)}, u32[]{:S(2)}) copy-start(f32[1,32]{1,0:T(1,128)} %shift_hbm.1) | copy-start | bytes 388
  7.1 0.7 %copy-start.7 = (f32[1,3]{1,0:T(1,128)S(1)}, f32[1,3]{1,0:T(1,128)}, u32[]{:S(2)}) copy-start(f32[1,3]{1,0:T(1,128)} %segb_hbm.1) | copy-start | bytes 40

commit v2 on v1

--- a/solution.py
+++ b/solution.py
@@ -44,10 +44,10 @@
 def kernel(
     depth, slabs,
     feat, cz_hbm, cy_hbm, cnt_hbm, w_hbm, gain_hbm, shift_hbm, segw_hbm, segb_hbm,
-    out_ref,
-    cz_ref, cy_ref, cnt_ref, w_ref, gain_ref, shift_ref, segw_ref, segb_ref, featv, staged, own, ints, ints_in, sendp, recvp, wall, prm, wa, wb, w9, seg, im, im9, hid,
+    out_hbm,
+    cz_ref, cy_ref, cnt_ref, w_ref, gain_ref, shift_ref, segw_ref, segb_ref, featv, out_ref, staged, own, ints, ints_in, sendp, recvp, wall, prm, wa, wb, w9, seg, im, im9, hid,
     sums, tsend, tin, tback, pad_in, pad_own, gpad, inv,
-    small_sem, feat_sem, int_s, int_r, pl_s, pl_r, w_s, w_r, p_s, p_r, a_s, a_r, b_s, b_r, c_s, c_r,
+    small_sem, feat_sem, out_sem, int_s, int_r, pl_s, pl_r, w_s, w_r, p_s, p_r, a_s, a_r, b_s, b_r, c_s, c_r,
 ):
     m = lax.axis_index("member")
     v = lax.axis_index("vol")
@@ -74,6 +74,15 @@
 
     for copy in small:
         copy.wait()
+
+    def chosen(ref_row):
+        value = ref_row(0)
+        for k in range(1, MAXP):
+            value = jnp.where(m == k, ref_row(k), value)
+        return value
+
+    my_z = chosen(lambda k: cz_ref[0, k])
+    my_y = chosen(lambda k: cy_ref[0, k])
 
     lane = lax.broadcasted_iota(jnp.int32, (8, X), 1)
     row = jnp.where(lane == 8, cnt_ref[0], 0)
@@ -118,21 +127,12 @@
         shared(wall, w_s, w_r, d).start()
         shared(prm, p_s, p_r, d).start()
 
-    def chosen(ref_row):
-        value = ref_row(0)
-        for k in range(1, MAXP):
-            value = jnp.where(m == k, ref_row(k), value)
-        return value
-
-    my_z = chosen(lambda k: cz_ref[0, k])
-    my_y = chosen(lambda k: cy_ref[0, k])
-    feat_copy.wait()
-
     def plane_copy(j):
         return pltpu.make_async_remote_copy(
             src_ref=sendp.at[j], dst_ref=recvp.at[j], send_sem=pl_s.at[j], recv_sem=pl_r.at[j],
             device_id=(m, nxt), device_id_type=MESH)
 
+    feat_copy.wait()
     for j in range(PZ):
         z = jnp.minimum(my_z + j, depth - 1)
 
@@ -374,15 +374,24 @@
         for k in range(K):
             out_ref[k, z] = powers[k] * whole
 
-    for z in range(PZ - 1):
-        finish(z, True)
-
     def rest(z, carry):
         finish(z, False)
         return carry
 
-    lax.fori_loop(PZ - 1, depth, rest, 0)
-
+    group = depth // 4
+    outs = [
+        pltpu.make_async_copy(
+            out_ref.at[:, pl.ds(g * group, group)], out_hbm.at[:, pl.ds(g * group, group)], out_sem.at[g])
+        for g in range(4)
+    ]
+    for z in range(PZ - 1):
+        finish(z, True)
+    for g in range(4):
+        lax.fori_loop(max(g * group, PZ - 1), (g + 1) * group, rest, 0)
+        outs[g].start()
+
+    for copy in outs:
+        copy.wait()
     int_copy.wait_send()
     for j in range(PZ):
         plane_copy(j).wait_send()
@@ -401,9 +410,9 @@
     return pl.pallas_call(
         functools.partial(kernel, depth, slabs),
         name="ensemble_patches",
-        out_shape=jax.ShapeDtypeStruct((K, depth, rows // M, width), f32),
+        out_shape=pltpu.HBM((K, depth, rows // M, width), f32),
         in_specs=[pl.BlockSpec(memory_space=pltpu.HBM)] * 9,
-        out_specs=pl.BlockSpec(memory_space=pltpu.VMEM),
+        out_specs=pl.BlockSpec(memory_space=pltpu.HBM),
         scratch_shapes=[
             pltpu.SMEM((1, MAXP), jnp.int32),
             pltpu.SMEM((1, MAXP), jnp.int32),
@@ -414,6 +423,7 @@
             pltpu.VMEM((1, K, C), bf16),
             pltpu.VMEM((1, K), f32),
             pltpu.VMEM((channels, depth, rows, width), bf16),
+            pltpu.VMEM((K, depth, rows // M, width), f32),
             pltpu.VMEM((C * rows, X), f32),
             pltpu.VMEM(((PZ - 1) * C * rows, X), f32),
             pltpu.VMEM((8, X), jnp.int32),
@@ -437,12 +447,14 @@
             pltpu.VMEM((MAXP, PZ + 2, K - 1, 24, X), f32),
             pltpu.VMEM((PZ + 2, 24, X), f32),
             pltpu.VMEM((depth, PY, X), f32),
-            dma((8,)), dma, dma, dma, dma((PZ,)), dma((PZ,)), dma((3,)), dma((3,)), dma((3,)), dma((3,)),
+            dma((8,)), dma, dma((4,)), dma, dma, dma((PZ,)), dma((PZ,)), dma((3,)), dma((3,)), dma((3,)), dma((3,)),
             dma((3,)), dma((3,)), dma, dma, dma((3,)), dma((3,)),
         ],
         compiler_params=pltpu.CompilerParams(
             collective_id=0, has_side_effects=True, vmem_limit_bytes=40 * 1024 * 1024),
-    )(features, corner_z, corner_y, counts, taps, norm_gain, norm_shift, seg_w, seg_b)
+    )(*[
+        arg if arg is counts else pltpu.with_memory_space_constraint(arg, pltpu.HBM)
+        for arg in (features, corner_z, corner_y, counts, taps, norm_gain, norm_shift, seg_w, seg_b)])
 
 
 def solution(mesh):

time: 33.9 us -> 28.3 us (0.83); the launches traced: 33.4 us -> 28.2 us
  local copies, waits for them, and re-layouts: 7.75 us -> 1.62 us
  Pallas kernels: 25 us -> 25.9 us
    unnamed x17 -> x1, local copies, waits for them, and re-layouts: 7.75 us -> 1.62 us
    pallas_call x1, Pallas kernels: 25 us -> 25.9 us  [per_device(): pl.pallas_call(functools.partial(kernel, depth, slabs), name='ensemble_pa...]
where the time goes in v2:
time: 28.3 us; the launch traced here: 28.2 us
  Pallas kernels  25.9 us (92%)
  local copies, waits for them, and re-layouts  1.62 us (6%)
  between operations  0.66 us (2%)
    pallas_call x1, Pallas kernels, per_device(): pl.pallas_call(functools.partial(kernel, depth, slabs), name='ensemble_pa...  25.9 us
    unnamed x1, local copies, waits for them, and re-layouts  1.62 us

profile of v2, /device:TPU:2, one launch (start us, length us, event | category | flops | bytes accessed | tf_op | source)
XLA Modules:
  0.0 28.2 jit_solution(17734719554472085976)
XLA Ops:
  0.7 25.9 %ensemble_patches.1 = f32[3,16,8,128]{3,2,1,0:T(8,128)} custom-call(bf16[32,16,32,128]{3,2,1,0:T(8,128)(2,1)} %feat.1, s32[1,4]{1,0:T(1,128)} %cz_hbm.1, s32[1,4]{1,0:T(1,128)} %cy_hbm.1, s32[1]{0:T(128)S(6)} %copy.11.cnt_hbm, bf16[3,3,3,32,32]{4,3,2,1,0:T(8,128)(2,1)} %bitcast.3, f32[1,32]{1,0:T(1,128)} %gain_hbm.1, f32[1,32]{1,0:T(1,128)} %shift_hbm.1, ...), custom_call_target="tpu_custom_call" | custom-call | tf_op jit(solution)/shard_map/ensemble_patches/pallas_call | solution.py:410
  26.6 1.6 %copy.12 = f32[3,16,8,128]{3,2,1,0:T(8,128)} copy(f32[3,16,8,128]{3,2,1,0:T(8,128)} %ensemble_patches.1) | data formatting | bytes 393216

commit v3 on v2

--- a/solution.py
+++ b/solution.py
@@ -44,10 +44,10 @@
 def kernel(
     depth, slabs,
     feat, cz_hbm, cy_hbm, cnt_hbm, w_hbm, gain_hbm, shift_hbm, segw_hbm, segb_hbm,
-    out_hbm,
-    cz_ref, cy_ref, cnt_ref, w_ref, gain_ref, shift_ref, segw_ref, segb_ref, featv, out_ref, staged, own, ints, ints_in, sendp, recvp, wall, prm, wa, wb, w9, seg, im, im9, hid,
+    out_ref,
+    cz_ref, cy_ref, cnt_ref, w_ref, gain_ref, shift_ref, segw_ref, segb_ref, featv, staged, own, ints, ints_in, sendp, recvp, wall, prm, wa, wb, w9, seg, im, im9, hid,
     sums, tsend, tin, tback, pad_in, pad_own, gpad, inv,
-    small_sem, feat_sem, out_sem, int_s, int_r, pl_s, pl_r, w_s, w_r, p_s, p_r, a_s, a_r, b_s, b_r, c_s, c_r,
+    small_sem, feat_sem, int_s, int_r, pl_s, pl_r, w_s, w_r, p_s, p_r, a_s, a_r, b_s, b_r, c_s, c_r,
 ):
     m = lax.axis_index("member")
     v = lax.axis_index("vol")
@@ -106,57 +106,6 @@
     prm[m, 2:5, 0:C] = segw_ref[0].astype(f32)
     prm[m, 5:6, 0:K] = segb_ref[...]
 
-    pl.semaphore_wait(barrier, 2 + len(mates))
-
-    int_copy = pltpu.make_async_remote_copy(
-        src_ref=ints, dst_ref=ints_in, send_sem=int_s, recv_sem=int_r,
-        device_id=(m, nxt), device_id_type=MESH)
-    int_copy.start()
-
-    def shared(buf, send, recv, d):
-        return pltpu.make_async_remote_copy(
-            src_ref=buf.at[m], dst_ref=buf.at[m], send_sem=send.at[d], recv_sem=recv.at[d],
-            device_id=(mates[d], v), device_id_type=MESH)
-
-    def arrives(buf, send, recv, d):
-        return pltpu.make_async_remote_copy(
-            src_ref=buf.at[froms[d]], dst_ref=buf.at[froms[d]], send_sem=send.at[d], recv_sem=recv.at[d],
-            device_id=(mates[d], v), device_id_type=MESH)
-
-    for d in range(M - 1):
-        shared(wall, w_s, w_r, d).start()
-        shared(prm, p_s, p_r, d).start()
-
-    def plane_copy(j):
-        return pltpu.make_async_remote_copy(
-            src_ref=sendp.at[j], dst_ref=recvp.at[j], send_sem=pl_s.at[j], recv_sem=pl_r.at[j],
-            device_id=(m, nxt), device_id_type=MESH)
-
-    feat_copy.wait()
-    for j in range(PZ):
-        z = jnp.minimum(my_z + j, depth - 1)
-
-        def stage(c, carry, z=z):
-            staged[pl.ds(c * rows, rows), :] = featv[c, z].astype(f32)
-            return carry
-
-        lax.fori_loop(0, C, stage, 0, unroll=8)
-
-        def pick(y, carry, j=j):
-            sendp[j, y] = staged[pl.ds(my_y + y, C, stride=rows), :].astype(bf16)
-            return carry
-
-        lax.fori_loop(0, PY, pick, 0, unroll=4)
-        plane_copy(j).start()
-
-    inside = (v > 0).astype(f32)
-    for j in range(PZ - 1):
-        def stage(c, carry, j=j):
-            own[pl.ds(j * C * rows + c * rows, rows), :] = featv[c, j].astype(f32) * inside
-            return carry
-
-        lax.fori_loop(0, C, stage, 0, unroll=8)
-
     for j in range(PZ):
         for kx in range(3):
             im[j * 256 + kx * C:j * 256 + (kx + 1) * C, X:2 * X] = jnp.zeros((C, X), bf16)
@@ -164,14 +113,6 @@
             t = 6 + kx
             im[j * 256 + t * C:j * 256 + (t + 1) * C, 8 * X:9 * X] = jnp.zeros((C, X), bf16)
         im9[j * C:(j + 1) * C, 8 * X:9 * X] = jnp.zeros((C, X), bf16)
-
-    int_copy.wait_recv()
-    got = ints_in[...]
-    prev_z = [jnp.sum(jnp.where(lane[0:1] == k, got[0:1], 0)) for k in range(MAXP)]
-    prev_y = [jnp.sum(jnp.where(lane[0:1] == 4 + k, got[0:1], 0)) for k in range(MAXP)]
-    prev_count = jnp.sum(jnp.where(lane[0:1] == 8, got[0:1], 0))
-    at_z = chosen(lambda k: prev_z[k])
-    at_y = chosen(lambda k: prev_y[k])
 
     gz, gy = bell(PZ), bell(PY)
     gyx = picked(gy, lax.broadcasted_iota(jnp.int32, (PY, X), 0)) * bell_x((PY, X))
@@ -188,6 +129,69 @@
                     pad[s, j, k, 16:24] = nothing
                     if j in (0, PZ + 1):
                         pad[s, j, k, 8:16] = nothing
+    wa[...] = jnp.zeros(wa.shape, bf16)
+    wb[...] = jnp.zeros(wb.shape, bf16)
+    w9[...] = jnp.zeros(w9.shape, bf16)
+    seg[...] = jnp.zeros(seg.shape, f32)
+
+    pl.semaphore_wait(barrier, 2 + len(mates))
+
+    int_copy = pltpu.make_async_remote_copy(
+        src_ref=ints, dst_ref=ints_in, send_sem=int_s, recv_sem=int_r,
+        device_id=(m, nxt), device_id_type=MESH)
+    int_copy.start()
+
+    def shared(buf, send, recv, d):
+        return pltpu.make_async_remote_copy(
+            src_ref=buf.at[m], dst_ref=buf.at[m], send_sem=send.at[d], recv_sem=recv.at[d],
+            device_id=(mates[d], v), device_id_type=MESH)
+
+    def arrives(buf, send, recv, d):
+        return pltpu.make_async_remote_copy(
+            src_ref=buf.at[froms[d]], dst_ref=buf.at[froms[d]], send_sem=send.at[d], recv_sem=recv.at[d],
+            device_id=(mates[d], v), device_id_type=MESH)
+
+    for d in range(M - 1):
+        shared(wall, w_s, w_r, d).start()
+        shared(prm, p_s, p_r, d).start()
+
+    def plane_copy(j):
+        return pltpu.make_async_remote_copy(
+            src_ref=sendp.at[j], dst_ref=recvp.at[j], send_sem=pl_s.at[j], recv_sem=pl_r.at[j],
+            device_id=(m, nxt), device_id_type=MESH)
+
+    feat_copy.wait()
+    for j in range(PZ):
+        z = jnp.minimum(my_z + j, depth - 1)
+
+        def stage(c, carry, z=z):
+            staged[pl.ds(c * rows, rows), :] = featv[c, z].astype(f32)
+            return carry
+
+        lax.fori_loop(0, C, stage, 0, unroll=8)
+
+        def pick(y, carry, j=j):
+            sendp[j, y] = staged[pl.ds(my_y + y, C, stride=rows), :].astype(bf16)
+            return carry
+
+        lax.fori_loop(0, PY, pick, 0, unroll=4)
+        plane_copy(j).start()
+
+    inside = (v > 0).astype(f32)
+    for j in range(PZ - 1):
+        def stage(c, carry, j=j):
+            own[pl.ds(j * C * rows + c * rows, rows), :] = featv[c, j].astype(f32) * inside
+            return carry
+
+        lax.fori_loop(0, C, stage, 0, unroll=8)
+
+    int_copy.wait_recv()
+    got = ints_in[...]
+    prev_z = [jnp.sum(jnp.where(lane[0:1] == k, got[0:1], 0)) for k in range(MAXP)]
+    prev_y = [jnp.sum(jnp.where(lane[0:1] == 4 + k, got[0:1], 0)) for k in range(MAXP)]
+    prev_count = jnp.sum(jnp.where(lane[0:1] == 8, got[0:1], 0))
+    at_z = chosen(lambda k: prev_z[k])
+    at_y = chosen(lambda k: prev_y[k])
 
     first = m * PY
     own_off = [8 + jnp.clip(first - cy_ref[0, k], -8, 8) for k in range(MAXP)]
@@ -206,14 +210,11 @@
         inv[z] = 1.0 / jnp.maximum(total, 0.1)
         return carry
 
-    lax.fori_loop(0, depth, weigh, 0)
+    lax.fori_loop(0, depth, weigh, 0, unroll=4)
 
     for d in range(M - 1):
         arrives(wall, w_s, w_r, d).wait_recv()
         arrives(prm, p_s, p_r, d).wait_recv()
-    wa[...] = jnp.zeros(wa.shape, bf16)
-    wb[...] = jnp.zeros(wb.shape, bf16)
-    w9[...] = jnp.zeros(w9.shape, bf16)
     for q in range(M):
         r = q * C
         full = wall[q, :, 0:768]
@@ -233,7 +234,6 @@
 
     gain = jnp.concatenate([column(prm[q, 0:1, 0:C]) for q in range(M)], axis=0)
     shift = jnp.concatenate([column(prm[q, 1:2, 0:C]) for q in range(M)], axis=0)
-    seg[...] = jnp.zeros(seg.shape, f32)
     for q in range(M):
         for o in range(2):
             at = o * 128 + q * C
@@ -282,7 +282,7 @@
             sums[...] += pair[:, :X] + pair[:, X:]
             return carry
 
-        lax.fori_loop(0, 4, conv, 0)
+        lax.fori_loop(0, 4, conv, 0, unroll=True)
 
     voxels = PZ * PY * X
     mean = jnp.sum(sums[...], axis=1, keepdims=True) / voxels
@@ -296,7 +296,7 @@
             sums[...] += pair[:, :X] + pair[:, X:]
             return carry
 
-        lax.fori_loop(0, 4, spread, 0)
+        lax.fori_loop(0, 4, spread, 0, unroll=True)
     variance = jnp.sum(sums[...], axis=1, keepdims=True) / voxels
     scale = lax.rsqrt(variance + 1e-05) * gain
 
@@ -324,7 +324,7 @@
                 tsend[p, pl.ds(y, 8, stride=8), :] = value
             return carry
 
-        lax.fori_loop(0, 4, classify, 0)
+        lax.fori_loop(0, 4, classify, 0, unroll=True)
 
     back = pltpu.make_async_remote_copy(
         src_ref=tsend.at[:, pl.ds(0, 32)], dst_ref=tback.at[m], send_sem=b_s, recv_sem=b_r,
@@ -378,20 +378,10 @@
         finish(z, False)
         return carry
 
-    group = depth // 4
-    outs = [
-        pltpu.make_async_copy(
-            out_ref.at[:, pl.ds(g * group, group)], out_hbm.at[:, pl.ds(g * group, group)], out_sem.at[g])
-        for g in range(4)
-    ]
     for z in range(PZ - 1):
         finish(z, True)
-    for g in range(4):
-        lax.fori_loop(max(g * group, PZ - 1), (g + 1) * group, rest, 0)
-        outs[g].start()
-
-    for copy in outs:
-        copy.wait()
+    lax.fori_loop(PZ - 1, depth, rest, 0, unroll=True)
+
     int_copy.wait_send()
     for j in range(PZ):
         plane_copy(j).wait_send()
@@ -410,9 +400,9 @@
     return pl.pallas_call(
         functools.partial(kernel, depth, slabs),
         name="ensemble_patches",
-        out_shape=pltpu.HBM((K, depth, rows // M, width), f32),
+        out_shape=jax.ShapeDtypeStruct((K, depth, rows // M, width), f32),
         in_specs=[pl.BlockSpec(memory_space=pltpu.HBM)] * 9,
-        out_specs=pl.BlockSpec(memory_space=pltpu.HBM),
+        out_specs=pl.BlockSpec(memory_space=pltpu.VMEM),
         scratch_shapes=[
             pltpu.SMEM((1, MAXP), jnp.int32),
             pltpu.SMEM((1, MAXP), jnp.int32),
@@ -423,7 +413,6 @@
             pltpu.VMEM((1, K, C), bf16),
             pltpu.VMEM((1, K), f32),
             pltpu.VMEM((channels, depth, rows, width), bf16),
-            pltpu.VMEM((K, depth, rows // M, width), f32),
             pltpu.VMEM((C * rows, X), f32),
             pltpu.VMEM(((PZ - 1) * C * rows, X), f32),
             pltpu.VMEM((8, X), jnp.int32),
@@ -447,7 +436,7 @@
             pltpu.VMEM((MAXP, PZ + 2, K - 1, 24, X), f32),
             pltpu.VMEM((PZ + 2, 24, X), f32),
             pltpu.VMEM((depth, PY, X), f32),
-            dma((8,)), dma, dma((4,)), dma, dma, dma((PZ,)), dma((PZ,)), dma((3,)), dma((3,)), dma((3,)), dma((3,)),
+            dma((8,)), dma, dma, dma, dma((PZ,)), dma((PZ,)), dma((3,)), dma((3,)), dma((3,)), dma((3,)),
             dma((3,)), dma((3,)), dma, dma, dma((3,)), dma((3,)),
         ],
         compiler_params=pltpu.CompilerParams(

time: 28.3 us -> 23.8 us (0.84)
  Pallas kernels: 25.9 us -> 22.3 us
  local copies, waits for them, and re-layouts: 1.62 us -> 0.68 us
    pallas_call x1, Pallas kernels: 25.9 us -> 22.3 us  [per_device(): pl.pallas_call(functools.partial(kernel, depth, slabs), name='ensemble_pa...]
    unnamed x1, local copies, waits for them, and re-layouts: 1.62 us -> 0.68 us
where the time goes in v3:
time: 23.8 us; the launch traced here: 23.7 us
  Pallas kernels  22.3 us (94%)
  local copies, waits for them, and re-layouts  0.68 us (3%)
  between operations  0.66 us (3%)
    pallas_call x1, Pallas kernels, per_device(): pl.pallas_call(functools.partial(kernel, depth, slabs), name='ensemble_pa...  22.3 us
    unnamed x1, local copies, waits for them, and re-layouts  0.68 us

profile of v3, /device:TPU:2, one launch (start us, length us, event | category | flops | bytes accessed | tf_op | source)
XLA Modules:
  0.0 23.7 jit_solution(13907492402563800843)
XLA Ops:
  0.7 22.3 %ensemble_patches.1 = f32[3,16,8,128]{3,2,1,0:T(8,128)S(1)} custom-call(bf16[32,16,32,128]{3,2,1,0:T(8,128)(2,1)} %feat.1, s32[1,4]{1,0:T(1,128)} %cz_hbm.1, s32[1,4]{1,0:T(1,128)} %cy_hbm.1, s32[1]{0:T(128)S(6)} %copy.11.cnt_hbm, bf16[3,3,3,32,32]{4,3,2,1,0:T(8,128)(2,1)} %bitcast.3, f32[1,32]{1,0:T(1,128)} %gain_hbm.1, f32[1,32]{1,0:T(1,128)} %shift_hbm.1, ...), custom_call_target="tpu_custom_call" | custom-call | tf_op jit(solution)/shard_map/ensemble_patches/pallas_call | solution.py:400
  23.0 0.7 %copy.12 = f32[3,16,8,128]{3,2,1,0:T(8,128)} copy(f32[3,16,8,128]{3,2,1,0:T(8,128)S(1)} %ensemble_patches.1) | data formatting | bytes 393216

commit v4 on v3

--- a/solution.py
+++ b/solution.py
@@ -168,13 +168,13 @@
             staged[pl.ds(c * rows, rows), :] = featv[c, z].astype(f32)
             return carry
 
-        lax.fori_loop(0, C, stage, 0, unroll=8)
+        lax.fori_loop(0, C, stage, 0, unroll=True)
 
         def pick(y, carry, j=j):
             sendp[j, y] = staged[pl.ds(my_y + y, C, stride=rows), :].astype(bf16)
             return carry
 
-        lax.fori_loop(0, PY, pick, 0, unroll=4)
+        lax.fori_loop(0, PY, pick, 0, unroll=True)
         plane_copy(j).start()
 
     inside = (v > 0).astype(f32)
@@ -183,7 +183,7 @@
             own[pl.ds(j * C * rows + c * rows, rows), :] = featv[c, j].astype(f32) * inside
             return carry
 
-        lax.fori_loop(0, C, stage, 0, unroll=8)
+        lax.fori_loop(0, C, stage, 0, unroll=True)
 
     int_copy.wait_recv()
     got = ints_in[...]
@@ -210,7 +210,7 @@
         inv[z] = 1.0 / jnp.maximum(total, 0.1)
         return carry
 
-    lax.fori_loop(0, depth, weigh, 0, unroll=4)
+    lax.fori_loop(0, depth, weigh, 0, unroll=True)
 
     for d in range(M - 1):
         arrives(wall, w_s, w_r, d).wait_recv()
@@ -269,7 +269,7 @@
                         im9[j * C:(j + 1) * C, at] = part
             return carry
 
-        lax.fori_loop(0, PY, expand, 0, unroll=2)
+        lax.fori_loop(0, PY, expand, 0, unroll=True)
 
     sums[...] = jnp.zeros(sums.shape, f32)
     for p, taps in enumerate((wa, wb)):

time: 23.8 us -> 23.4 us (0.983)
  Pallas kernels: 22.3 us -> 22 us
    pallas_call x1, Pallas kernels: 22.3 us -> 22 us  [per_device(): pl.pallas_call(functools.partial(kernel, depth, slabs), name='ensemble_pa...]
where the time goes in v4:
time: 23.4 us; the launch traced here: 23.3 us
  Pallas kernels  22 us (94%)
  local copies, waits for them, and re-layouts  0.68 us (3%)
  between operations  0.66 us (3%)
    pallas_call x1, Pallas kernels, per_device(): pl.pallas_call(functools.partial(kernel, depth, slabs), name='ensemble_pa...  22 us
    unnamed x1, local copies, waits for them, and re-layouts  0.68 us

profile of v4, /device:TPU:2, one launch (start us, length us, event | category | flops | bytes accessed | tf_op | source)
XLA Modules:
  0.0 23.3 jit_solution(13616617020561876466)
XLA Ops:
  0.7 22.0 %ensemble_patches.1 = f32[3,16,8,128]{3,2,1,0:T(8,128)S(1)} custom-call(bf16[32,16,32,128]{3,2,1,0:T(8,128)(2,1)} %feat.1, s32[1,4]{1,0:T(1,128)} %cz_hbm.1, s32[1,4]{1,0:T(1,128)} %cy_hbm.1, s32[1]{0:T(128)S(6)} %copy.11.cnt_hbm, bf16[3,3,3,32,32]{4,3,2,1,0:T(8,128)(2,1)} %bitcast.3, f32[1,32]{1,0:T(1,128)} %gain_hbm.1, f32[1,32]{1,0:T(1,128)} %shift_hbm.1, ...), custom_call_target="tpu_custom_call" | custom-call | tf_op jit(solution)/shard_map/ensemble_patches/pallas_call | solution.py:400
  22.6 0.7 %copy.12 = f32[3,16,8,128]{3,2,1,0:T(8,128)} copy(f32[3,16,8,128]{3,2,1,0:T(8,128)S(1)} %ensemble_patches.1) | data formatting | bytes 393216
